TPU v7x, 256 devices: a whole 4x4x8 slice. The times are simulated.
256 devices in a mesh: stream: 2 (over z_hi), dp: 16 (over x, y), tensor: 8 (over z_lo, core).
Axes of the slice: x: 4, y: 4, z: 8 (z_hi: 2, z_lo: 4; z = z_hi * 4 + z_lo), core: 2. Of those that a mesh axis runs over, the one named last changes fastest.
Arguments:
- hidden: bfloat16 [2, 256, 8192], P('stream', 'tensor', 'dp'), may hold values from -3 to 3
- cached_rotated_keys: bfloat16 [2, 256, 8, 256, 128], P('stream', 'dp', 'tensor'), may hold values from -6 to 6
- cached_values: bfloat16 [2, 256, 8, 256, 128], P('stream', 'dp', 'tensor'), may hold values from -18 to 18
- cache_lengths: int32 [2, 256], P('stream', 'dp'), may hold values from 1 to 256, as said below
- recent_ids: int32 [256, 128], replicated, may hold values from 0 to 65535
- guidance: float32 [256], replicated, may hold values from 1 to 3
- w_query: bfloat16 [8192, 8192], P('dp', 'tensor'), may hold values from -0.0625 to 0.0625
- key_value_weight: bfloat16 [8192, 2, 1024], P('dp', None, 'tensor'), may hold values from -0.0625 to 0.0625
- w_output: bfloat16 [8192, 8192], P('tensor', 'dp'), may hold values from -0.0625 to 0.0625
- norm_gain: bfloat16 [8192], P('dp'), may hold values from 0.5 to 1.5
- w_head: bfloat16 [8192, 65536], P(None, ('dp', 'tensor')), may hold values from -0.16503906 to 0.16503906
Outputs:
- guided_logprobs: float32 [256, 65536], P('stream', ('dp', 'tensor'))
Inputs may be any that keep to these rules, and one draw needn't show every extreme that they name: `cache_lengths`: every prompt has 1 to 256 filled slots in each stream; some prompt has all 256; lengths differ widely from one group of 16 prompts to the next.
All inputs are finite; a program needn't handle non-finite values.
Results may differ from a plain program's by a relative error of at most 0.0025.
Values may be sent and summed in bfloat16 or wider, within the bound.
A program may use at most 64 MiB of HBM per device.

v0:
```python
import jax
import jax.numpy as jnp
from jax import lax
from jax.sharding import PartitionSpec as P

MODEL_WIDTH = 8192
HEAD_SIZE = 128
rope_theta = 500000.0
penalty_step = 1.5
norm_eps = 1e-05


def partner_2(value, axis, distance):
    mask = 2**distance
    pairs = [(source, source ^ mask) for source in range(lax.axis_size(axis))]
    return lax.ppermute(value, axis, pairs)


def rotate(values, positions):
    halfway = values.shape[-1] // 2
    frequency = rope_theta ** (-(jnp.arange(halfway, dtype=jnp.float32) * 2.0 / values.shape[-1]))
    angles = positions.astype(jnp.float32)[:, None, None] * frequency
    cosine_term = jnp.cos(angles)
    sine_term = jnp.sin(angles)
    first_half = values[..., :halfway]
    second_half = values[..., halfway:]
    return jnp.concatenate(
        [
            first_half * cosine_term - second_half * sine_term,
            second_half * cosine_term + first_half * sine_term,
        ],
        axis=-1,
    )


def repeat_counts(recent_ids, first_column, width):
    columns = first_column + jnp.arange(width, dtype=jnp.int32)
    return jnp.sum((recent_ids[:, :, None] == columns[None, None, :]).astype(jnp.float32), 1)


def body(
    hidden,
    cached_rotated_keys,
    cached_values,
    cache_lengths,
    recent_ids,
    guidance,
    w_query,
    key_value_weight,
    w_output,
    norm_gain,
    w_head,
):
    local_width = hidden.shape[2]
    query_cols = w_query.shape[1]
    kv_cols = key_value_weight.shape[2]
    local_prompts = cache_lengths.shape[1]
    lengths = cache_lengths[0]
    vocab_local = w_head.shape[1]
    all_rows = lax.all_gather(hidden[0], "tensor", axis=0, tiled=True)
    kv_flat = key_value_weight.reshape(local_width, 2 * kv_cols)
    projected = lax.psum_scatter(
        jnp.concatenate(
            [
                jnp.dot(all_rows, w_query, preferred_element_type=jnp.float32),
                jnp.dot(all_rows, kv_flat, preferred_element_type=jnp.float32),
            ],
            axis=1,
        ),
        "dp",
        scatter_dimension=0,
        tiled=True,
    )
    query_heads = query_cols // HEAD_SIZE
    kv_heads = kv_cols // HEAD_SIZE
    rotated_query = rotate(
        projected[:, :query_cols].reshape(local_prompts, query_heads, HEAD_SIZE), lengths
    ).astype(jnp.bfloat16)
    key_value_rows = projected[:, query_cols:].reshape(local_prompts, 2, kv_heads, HEAD_SIZE)
    fresh_key = rotate(key_value_rows[:, 0], lengths).astype(jnp.bfloat16)
    value_new = key_value_rows[:, 1].astype(jnp.bfloat16)
    grouped_queries = rotated_query.reshape(
        local_prompts, kv_heads, query_heads // kv_heads, HEAD_SIZE
    )
    attention_scale = HEAD_SIZE ** (-0.5)
    key_block = cached_rotated_keys[0]
    value_block = cached_values[0]
    scores = (
        jnp.einsum(
            "pkgd,pksd->pkgs", grouped_queries, key_block, preferred_element_type=jnp.float32
        )
        * attention_scale
    )
    self_score = (
        jnp.einsum("pkgd,pkd->pkg", grouped_queries, fresh_key, preferred_element_type=jnp.float32)
        * attention_scale
    )
    valid = jnp.arange(key_block.shape[2], dtype=jnp.int32)[None, :] < lengths[:, None]
    exps = jnp.where(valid[:, None, None, :], jnp.exp(scores), 0.0)
    own_exp = jnp.exp(self_score)
    denominator = jnp.sum(exps, -1) + own_exp
    weights = (exps / denominator[..., None]).astype(jnp.bfloat16)
    own_weight = (own_exp / denominator).astype(jnp.bfloat16)
    attended = jnp.einsum(
        "pkgs,pksd->pkgd", weights, value_block, preferred_element_type=jnp.float32
    )
    attended = (
        attended
        + own_weight.astype(jnp.float32)[..., None] * value_new.astype(jnp.float32)[:, :, None, :]
    )
    attended = attended.reshape(local_prompts, query_cols).astype(jnp.bfloat16)
    partial_out = jnp.dot(
        lax.all_gather(attended, "dp", axis=0, tiled=True),
        w_output,
        preferred_element_type=jnp.float32,
    )
    output_sum = lax.psum_scatter(partial_out, "tensor", scatter_dimension=0, tiled=True)
    residual = (hidden[0].astype(jnp.float32) + output_sum).astype(jnp.bfloat16)
    widened = residual.astype(jnp.float32)
    squares = lax.psum(jnp.sum(widened * widened, 1), "dp")
    inverse = lax.rsqrt(squares / MODEL_WIDTH + norm_eps)
    normed = (widened * inverse[:, None] * norm_gain.astype(jnp.float32)).astype(jnp.bfloat16)
    normed_all = lax.all_gather(normed, "tensor", axis=0, tiled=True)
    logits = jnp.dot(
        lax.all_gather(normed_all, "dp", axis=1, tiled=True),
        w_head,
        preferred_element_type=jnp.float32,
    )
    stream_side = lax.axis_index("stream")
    half_rows = logits.shape[0] // 2
    mine_start = stream_side * half_rows
    other_start = (1 - stream_side) * half_rows
    column_base = lax.axis_index(("dp", "tensor")) * vocab_local
    mine = lax.dynamic_slice_in_dim(logits, mine_start, half_rows, 0)
    sending = lax.dynamic_slice_in_dim(logits, other_start, half_rows, 0)
    partner = partner_2(sending, "stream", 0)
    conditional = jnp.where(stream_side == 0, mine, partner)
    unconditional = jnp.where(stream_side == 0, partner, mine)
    guide = lax.dynamic_slice_in_dim(guidance, mine_start, half_rows, 0)[:, None]
    recent_mine = lax.dynamic_slice_in_dim(recent_ids, mine_start, half_rows, 0)
    guided = unconditional + guide * (conditional - unconditional)
    guided = guided - penalty_step * repeat_counts(recent_mine, column_base, vocab_local)
    totals = lax.psum(jnp.sum(jnp.exp(guided), 1), ("dp", "tensor"))
    return guided - jnp.log(totals)[:, None]


def solution(mesh):
    return jax.shard_map(
        body,
        mesh=mesh,
        in_specs=(
            P("stream", "tensor", "dp"),
            P("stream", "dp", "tensor", None, None),
            P("stream", "dp", "tensor", None, None),
            P("stream", "dp"),
            P(),
            P(),
            P("dp", "tensor"),
            P("dp", None, "tensor"),
            P("tensor", "dp"),
            P("dp"),
            P(None, ("dp", "tensor")),
        ),
        out_specs=P("stream", ("dp", "tensor")),
        check_vma=False,
    )
```

profile of v0, /device:TPU:128, one launch (start us, length us, event | category | flops | bytes accessed | tf_op | source)
XLA Modules:
  0.0 647.4 jit_solution(1154850240006349418)
XLA Ops:
  6.6 14.5 %all-gather = bf16[1,256,512]{2,1,0:T(8,128)(2,1)S(1)} all-gather(bf16[1,32,512]{2,1,0:T(8,128)(2,1)} %param.11), channel_id=2, replica_groups=mesh['stream'=2,'dp'=16,'tensor'=8] {'tensor'}, dimensions={1}, use_global_device_ids=true | all-gather | bytes 294912 | tf_op jit(solution)/shard_map/all_gather | solution.py:60
  21.1 0.5 fusion.9
  21.6 1.2 fusion.5
  22.8 1.2 pad_maximum_fusion
  24.1 0.7 bitcast_convert_fusion
  24.7 0.7 iota_compare_fusion
  25.4 0.1 multiply_cosine_fusion.1
  25.6 79.2 %reduce-scatter.3.cloned.1.call-done = f32[16,1280]{1,0:T(8,128)} async-done(((f32[256,1280]{1,0:T(8,128)}), f32[16,1280]{1,0:T(8,128)}) %reduce-scatter.3.cloned.1.call-update) | async-done | bytes 81936 | tf_op jit(solution)/shard_map/reduce_scatter | solution.py:62
  104.8 0.7 slice.36
  105.6 0.1 fusion.30
  105.7 0.8 slice_bitcast_fusion
  106.6 0.1 maximum_bitcast_fusion
  106.6 0.1 subtract_convert_fusion
  106.7 0.2 fusion.25
  106.9 1.7 fusion.33
  108.7 0.3 fusion.2
  109.0 23.3 %all_gather.13 = bf16[256,1024]{1,0:T(8,128)(2,1)S(1)} all-gather(bf16[16,1024]{1,0:T(8,128)(2,1)S(1)} %bitcast.51), channel_id=1, replica_groups=mesh['stream'=2,'dp'=16,'tensor'=8] {'dp'}, dimensions={0}, use_global_device_ids=true | all-gather | bytes 557056 | tf_op jit(solution)/shard_map/all_gather | solution.py:113
  132.3 1.2 fusion.34
  133.6 32.9 %reduce-scatter.5.cloned.1.call-done = f32[32,512]{1,0:T(8,128)} async-done(((f32[256,512]{1,0:T(8,128)}), f32[32,512]{1,0:T(8,128)}) %reduce-scatter.5.cloned.1.call-update) | async-done | bytes 65552 | tf_op jit(solution)/shard_map/reduce_scatter | solution.py:117
  166.5 1.0 fusion.11
  167.5 40.3 %psum.14 = f32[32]{0:T(128)S(1)} all-reduce(f32[32]{0:T(128)S(1)} %fusion.11), channel_id=1, replica_groups=mesh['stream'=2,'dp'=16,'tensor'=8] {'dp'}, use_global_device_ids=true, to_apply=%region_4.5 | all-reduce | flops 32 | bytes 256 | tf_op jit(solution)/shard_map/psum | solution.py:120
  207.8 0.9 fusion.13
  208.7 15.3 %all_gather.14 = bf16[256,512]{1,0:T(8,128)(2,1)} all-gather(bf16[32,512]{1,0:T(8,128)(2,1)S(1)} %fusion.13), channel_id=1, replica_groups=mesh['stream'=2,'dp'=16,'tensor'=8] {'tensor'}, dimensions={0}, use_global_device_ids=true | all-gather | bytes 294912 | tf_op jit(solution)/shard_map/all_gather | solution.py:123
  224.1 0.1 dynamic_slice.14
  224.2 58.3 %all-gather.3.cloned.1.call-done = bf16[256,8192]{1,0:T(8,128)(2,1)} async-done(((bf16[256,512]{1,0:T(8,128)(2,1)}), bf16[256,8192]{1,0:T(8,128)(2,1)}) %all-gather.3.cloned.1.call-update) | async-done | bytes 4194320 | tf_op jit(solution)/shard_map/all_gather | solution.py:125
  282.5 7.0 %fusion.35 = f32[256,512]{1,0:T(8,128)S(1)} fusion(bf16[256,8192]{1,0:T(8,128)(2,1)} %all-gather.3.cloned.1.call-done, bf16[8192,512]{1,0:T(8,128)(2,1)} %param.21), kind=kOutput, calls=%fused_computation.66 | convolution fusion | flops 2147483648 | bytes 13107200 | tf_op jit(solution)/shard_map/dot_general | solution.py:124
  289.5 0.3 collective-permute-start
  289.8 4.7 convert_reduce_fusion
  294.4 11.4 %collective-permute-done = f32[128,512]{1,0:T(8,128)S(1)} collective-permute-done((f32[128,512]{1,0:T(8,128)S(1)}, f32[128,512]{1,0:T(8,128)S(1)}, u32[]{:S(2)}, u32[]{:S(2)}) %collective-permute-start) | collective-permute-done | bytes 262176 | tf_op jit(solution)/shard_map/ppermute | solution.py:16
  305.8 0.2 exponential_reduce_fusion
  306.0 334.1 %psum.15 = f32[128]{0:T(128)S(1)} all-reduce(f32[128]{0:T(128)S(1)} %get-tuple-element.5), channel_id=1, replica_groups=mesh['stream'=2,'dp'=16,'tensor'=8] {'dp','tensor'}, use_global_device_ids=true, to_apply=%region_7.8 | all-reduce | flops 128 | bytes 1024 | tf_op jit(solution)/shard_map/psum | solution.py:143
  640.1 0.8 broadcast_subtract_fusion
  (33 shorter events, 0.3 us)
Async XLA Ops:
  6.5 14.6 %copy-start = (bf16[512,1024]{1,0:T(8,128)(2,1)S(1)}, bf16[512,1024]{1,0:T(8,128)(2,1)}, u32[]{:S(2)}) copy-start(bf16[512,1024]{1,0:T(8,128)(2,1)} %param.17) | copy-start | bytes 3145732
  6.5 160.0 %copy-start.3 = (bf16[1,32,512]{2,1,0:T(8,128)(2,1)S(1)}, bf16[1,32,512]{2,1,0:T(8,128)(2,1)}, u32[]{:S(2)}) copy-start(bf16[1,32,512]{2,1,0:T(8,128)(2,1)} %param.11) | copy-start | bytes 98308
  6.5 102.2 %copy-start.1 = (bf16[1,16,1,256,128]{4,3,2,1,0:T(8,128)(2,1)S(1)}, bf16[1,16,1,256,128]{4,3,2,1,0:T(8,128)(2,1)}, u32[]{:S(2)}) copy-start(bf16[1,16,1,256,128]{4,3,2,1,0:T(8,128)(2,1)} %param.13) | copy-start | bytes 3145732
  6.5 125.8 %copy-start.2 = (bf16[1024,512]{1,0:T(8,128)(2,1)S(1)}, bf16[1024,512]{1,0:T(8,128)(2,1)}, u32[]{:S(2)}) copy-start(bf16[1024,512]{1,0:T(8,128)(2,1)} %param.19) | copy-start | bytes 3145732
  6.5 127.1 %copy-start.5 = (bf16[512]{0:T(512)(128)(2,1)S(1)}, bf16[512]{0:T(512)(128)(2,1)}, u32[]{:S(2)}) copy-start(bf16[512]{0:T(512)(128)(2,1)} %param.20) | copy-start | bytes 3076
  6.5 217.5 %copy-start.6 = (f32[256]{0:T(256)S(1)}, f32[256]{0:T(256)}, u32[]{:S(2)}) copy-start(f32[256]{0:T(256)} %param.16) | copy-start | bytes 3076
  6.6 217.6 %copy-start.4 = (s32[256,128]{1,0:T(8,128)S(1)}, s32[256,128]{1,0:T(8,128)}, u32[]{:S(2)}) copy-start(s32[256,128]{1,0:T(8,128)} %param.15) | copy-start | bytes 393220
  6.6 98.2 %reduce-scatter.3.cloned.1.call-start = ((), (), s32[]{:S(2)}) async-start(), calls=%async_computation.2 | async-start | bytes 1392640 | tf_op jit(solution)/shard_map/reduce_scatter | solution.py:62
  24.0 142.5 %reduce-scatter.5.cloned.1.call-start = ((), (), s32[]{:S(2)}) async-start(), calls=%async_computation.3 | async-start | bytes 589824 | tf_op jit(solution)/shard_map/reduce_scatter | solution.py:117
  133.6 148.9 %all-gather.3.cloned.1.call-start = ((), (), s32[]{:S(2)}) async-start(), calls=%async_computation.4 | async-start | bytes 4456448 | tf_op jit(solution)/shard_map/all_gather | solution.py:125
  289.5 16.3 %collective-permute-start = (f32[128,512]{1,0:T(8,128)S(1)}, f32[128,512]{1,0:T(8,128)S(1)}, u32[]{:S(2)}, u32[]{:S(2)}) collective-permute-start(f32[128,512]{1,0:T(8,128)S(1)} %constant_dynamic-slice_fusion.1), channel_id=1, source_target_pairs={{0,128},{128,0},{1,129},{129,1},{2,130},{130,2},{3,131},{131,3},{4... | collective-permute-start | bytes 786440 | tf_op jit(solution)/shard_map/ppermute | solution.py:16
Sparse Core Ops, SparseCore 0:
  24.1 80.6 reduce-scatter.2
  133.7 32.7 reduce-scatter.4
  224.2 58.2 all-gather.2
where the time goes:
time: 648 us; the launch traced here: 647 us
  blocking collectives  427 us (66%)
  waiting for transfers between devices  182 us (28%)
  between operations  13.3 us (2%)
  matrix products  12.1 us (2%)
  other arithmetic  10.5 us (2%)
    psum x1, blocking collectives, body(): totals = lax.psum(jnp.sum(jnp.exp(guided), 1), ('dp', 'tensor'))  334 us
    reduce_scatter x1, waiting for transfers between devices, body(): lax.psum_scatter(jnp.concatenate([jnp.dot(all_rows, w_query, preferred_el...  79.2 us
    all_gather x1, waiting for transfers between devices, body(): lax.all_gather(normed_all, 'dp', axis=1, tiled=True)  58.3 us
    psum x1, blocking collectives, body(): squares = lax.psum(jnp.sum(widened * widened, 1), 'dp')  40.3 us
    reduce_scatter x1, waiting for transfers between devices, body(): lax.psum_scatter(partial_out, 'tensor', scatter_dimension=0, tiled=True)  32.9 us
    all_gather x1, blocking collectives, body(): lax.all_gather(attended, 'dp', axis=0, tiled=True)  23.3 us
    all_gather x1, blocking collectives, body(): normed_all = lax.all_gather(normed, 'tensor', axis=0, tiled=True)  15.3 us
    all_gather x1, blocking collectives, body(): all_rows = lax.all_gather(hidden[0], 'tensor', axis=0, tiled=True)  14.5 us
  transfers between devices with their start and end apart: 4, of which 4 were waited for; matrix products, arithmetic and copies ran while one was open for 1% of the time, Pallas kernels for 0%

commit v1 on v0

--- a/solution.py
+++ b/solution.py
@@ -140,7 +140,7 @@
     recent_mine = lax.dynamic_slice_in_dim(recent_ids, mine_start, half_rows, 0)
     guided = unconditional + guide * (conditional - unconditional)
     guided = guided - penalty_step * repeat_counts(recent_mine, column_base, vocab_local)
-    totals = lax.psum(jnp.sum(jnp.exp(guided), 1), ("dp", "tensor"))
+    totals = lax.psum(lax.psum(jnp.sum(jnp.exp(guided), 1), "dp"), "tensor")
     return guided - jnp.log(totals)[:, None]
 
 

time: 648 us -> 367 us (0.57)
  blocking collectives: 427 us -> 145 us
    psum x1 -> x2, blocking collectives: 334 us -> 51.7 us  [body(): totals = lax.psum(lax.psum(jnp.sum(jnp.exp(guided), 1), 'dp'), 'tensor')]
  transfers between devices with their start and end apart: 4 -> 4, of which waited for: 4 -> 4; matrix products, arithmetic and copies ran while one was open for 1% -> 2% of each run, Pallas kernels for 0% -> 0%
where the time goes in v1:
time: 367 us; the launch traced here: 365 us
  waiting for transfers between devices  182 us (50%)
  blocking collectives  145 us (40%)
  between operations  13.3 us (4%)
  matrix products  12.1 us (3%)
  other arithmetic  10.5 us (3%)
    reduce_scatter x1, waiting for transfers between devices, body(): lax.psum_scatter(jnp.concatenate([jnp.dot(all_rows, w_query, preferred_el...  79.2 us
    all_gather x1, waiting for transfers between devices, body(): lax.all_gather(normed_all, 'dp', axis=1, tiled=True)  58.3 us
    psum x2, blocking collectives, body(): totals = lax.psum(lax.psum(jnp.sum(jnp.exp(guided), 1), 'dp'), 'tensor')  51.7 us
    psum x1, blocking collectives, body(): squares = lax.psum(jnp.sum(widened * widened, 1), 'dp')  40.3 us
    reduce_scatter x1, waiting for transfers between devices, body(): lax.psum_scatter(partial_out, 'tensor', scatter_dimension=0, tiled=True)  32.9 us
    all_gather x1, blocking collectives, body(): lax.all_gather(attended, 'dp', axis=0, tiled=True)  23.3 us
    all_gather x1, blocking collectives, body(): normed_all = lax.all_gather(normed, 'tensor', axis=0, tiled=True)  15.3 us
    all_gather x1, blocking collectives, body(): all_rows = lax.all_gather(hidden[0], 'tensor', axis=0, tiled=True)  14.5 us
  transfers between devices with their start and end apart: 4, of which 4 were waited for; matrix products, arithmetic and copies ran while one was open for 2% of the time, Pallas kernels for 0%

profile of v1, /device:TPU:128, one launch (start us, length us, event | category | flops | bytes accessed | tf_op | source)
XLA Modules:
  0.0 365.1 jit_solution(14583464911725139870)
XLA Ops:
  6.6 14.5 %all-gather = bf16[1,256,512]{2,1,0:T(8,128)(2,1)S(1)} all-gather(bf16[1,32,512]{2,1,0:T(8,128)(2,1)} %param.11), channel_id=2, replica_groups=mesh['stream'=2,'dp'=16,'tensor'=8] {'tensor'}, dimensions={1}, use_global_device_ids=true | all-gather | bytes 294912 | tf_op jit(solution)/shard_map/all_gather | solution.py:60
  21.1 0.5 fusion.9
  21.6 1.2 fusion.5
  22.8 1.2 pad_maximum_fusion
  24.1 0.7 bitcast_convert_fusion
  24.7 0.7 iota_compare_fusion
  25.4 0.1 multiply_cosine_fusion.1
  25.6 79.2 %reduce-scatter.3.cloned.1.call-done = f32[16,1280]{1,0:T(8,128)} async-done(((f32[256,1280]{1,0:T(8,128)}), f32[16,1280]{1,0:T(8,128)}) %reduce-scatter.3.cloned.1.call-update) | async-done | bytes 81936 | tf_op jit(solution)/shard_map/reduce_scatter | solution.py:62
  104.8 0.7 slice.36
  105.6 0.1 fusion.30
  105.7 0.8 slice_bitcast_fusion
  106.6 0.1 subtract_convert_fusion
  106.7 0.2 fusion.25
  106.9 1.7 fusion.33
  108.7 0.3 fusion.2
  109.0 23.3 %all_gather.13 = bf16[256,1024]{1,0:T(8,128)(2,1)S(1)} all-gather(bf16[16,1024]{1,0:T(8,128)(2,1)S(1)} %bitcast.51), channel_id=1, replica_groups=mesh['stream'=2,'dp'=16,'tensor'=8] {'dp'}, dimensions={0}, use_global_device_ids=true | all-gather | bytes 557056 | tf_op jit(solution)/shard_map/all_gather | solution.py:113
  132.3 1.2 fusion.34
  133.6 32.9 %reduce-scatter.5.cloned.1.call-done = f32[32,512]{1,0:T(8,128)} async-done(((f32[256,512]{1,0:T(8,128)}), f32[32,512]{1,0:T(8,128)}) %reduce-scatter.5.cloned.1.call-update) | async-done | bytes 65552 | tf_op jit(solution)/shard_map/reduce_scatter | solution.py:117
  166.5 1.0 fusion.11
  167.5 40.3 %psum.21 = f32[32]{0:T(128)S(1)} all-reduce(f32[32]{0:T(128)S(1)} %fusion.11), channel_id=1, replica_groups=mesh['stream'=2,'dp'=16,'tensor'=8] {'dp'}, use_global_device_ids=true, to_apply=%region_4.5 | all-reduce | flops 32 | bytes 256 | tf_op jit(solution)/shard_map/psum | solution.py:120
  207.8 0.9 fusion.13
  208.7 15.3 %all_gather.14 = bf16[256,512]{1,0:T(8,128)(2,1)} all-gather(bf16[32,512]{1,0:T(8,128)(2,1)S(1)} %fusion.13), channel_id=1, replica_groups=mesh['stream'=2,'dp'=16,'tensor'=8] {'tensor'}, dimensions={0}, use_global_device_ids=true | all-gather | bytes 294912 | tf_op jit(solution)/shard_map/all_gather | solution.py:123
  224.1 0.1 dynamic_slice.14
  224.2 58.3 %all-gather.3.cloned.1.call-done = bf16[256,8192]{1,0:T(8,128)(2,1)} async-done(((bf16[256,512]{1,0:T(8,128)(2,1)}), bf16[256,8192]{1,0:T(8,128)(2,1)}) %all-gather.3.cloned.1.call-update) | async-done | bytes 4194320 | tf_op jit(solution)/shard_map/all_gather | solution.py:125
  282.5 7.0 %fusion.35 = f32[256,512]{1,0:T(8,128)S(1)} fusion(bf16[256,8192]{1,0:T(8,128)(2,1)} %all-gather.3.cloned.1.call-done, bf16[8192,512]{1,0:T(8,128)(2,1)} %param.21), kind=kOutput, calls=%fused_computation.66 | convolution fusion | flops 2147483648 | bytes 13107200 | tf_op jit(solution)/shard_map/dot_general | solution.py:124
  289.5 0.3 collective-permute-start
  289.8 4.7 %convert_reduce_fusion = f32[128,512]{1,0:T(8,128)S(1)} fusion(s32[512]{0:T(512)S(1)} %iota_add_fusion, s32[128,128]{1,0:T(8,128)S(1)} %constant_dynamic-slice_fusion), kind=kLoop, calls=%fused_computation | loop fusion | flops 25100288 | bytes 329728 | tf_op jit(solution)/shard_map/reduce_sum | solution.py:38
  294.4 11.4 %collective-permute-done = f32[128,512]{1,0:T(8,128)S(1)} collective-permute-done((f32[128,512]{1,0:T(8,128)S(1)}, f32[128,512]{1,0:T(8,128)S(1)}, u32[]{:S(2)}, u32[]{:S(2)}) %collective-permute-start) | collective-permute-done | bytes 262176 | tf_op jit(solution)/shard_map/ppermute | solution.py:16
  305.8 0.2 exponential_reduce_fusion
  306.0 38.1 %psum.22 = f32[128]{0:T(128)S(1)} all-reduce(f32[128]{0:T(128)S(1)} %get-tuple-element.5), channel_id=1, replica_groups=mesh['stream'=2,'dp'=16,'tensor'=8] {'dp'}, use_global_device_ids=true, to_apply=%region_7.8 | all-reduce | flops 128 | bytes 1024 | tf_op jit(solution)/shard_map/psum | solution.py:143
  344.1 13.6 %psum.23 = f32[128]{0:T(128)S(1)} all-reduce(f32[128]{0:T(128)S(1)} %psum.22), channel_id=1, replica_groups=mesh['stream'=2,'dp'=16,'tensor'=8] {'tensor'}, use_global_device_ids=true, to_apply=%region_8.9 | all-reduce | flops 128 | bytes 1024 | tf_op jit(solution)/shard_map/psum | solution.py:143
  357.7 0.8 broadcast_subtract_fusion
  (34 shorter events, 0.4 us)
Async XLA Ops:
  6.5 14.6 %copy-start = (bf16[512,1024]{1,0:T(8,128)(2,1)S(1)}, bf16[512,1024]{1,0:T(8,128)(2,1)}, u32[]{:S(2)}) copy-start(bf16[512,1024]{1,0:T(8,128)(2,1)} %param.17) | copy-start | bytes 3145732
  6.5 160.0 %copy-start.3 = (bf16[1,32,512]{2,1,0:T(8,128)(2,1)S(1)}, bf16[1,32,512]{2,1,0:T(8,128)(2,1)}, u32[]{:S(2)}) copy-start(bf16[1,32,512]{2,1,0:T(8,128)(2,1)} %param.11) | copy-start | bytes 98308
  6.5 102.2 %copy-start.1 = (bf16[1,16,1,256,128]{4,3,2,1,0:T(8,128)(2,1)S(1)}, bf16[1,16,1,256,128]{4,3,2,1,0:T(8,128)(2,1)}, u32[]{:S(2)}) copy-start(bf16[1,16,1,256,128]{4,3,2,1,0:T(8,128)(2,1)} %param.13) | copy-start | bytes 3145732
  6.5 125.8 %copy-start.2 = (bf16[1024,512]{1,0:T(8,128)(2,1)S(1)}, bf16[1024,512]{1,0:T(8,128)(2,1)}, u32[]{:S(2)}) copy-start(bf16[1024,512]{1,0:T(8,128)(2,1)} %param.19) | copy-start | bytes 3145732
  6.5 127.1 %copy-start.5 = (bf16[512]{0:T(512)(128)(2,1)S(1)}, bf16[512]{0:T(512)(128)(2,1)}, u32[]{:S(2)}) copy-start(bf16[512]{0:T(512)(128)(2,1)} %param.20) | copy-start | bytes 3076
  6.5 217.5 %copy-start.6 = (f32[256]{0:T(256)S(1)}, f32[256]{0:T(256)}, u32[]{:S(2)}) copy-start(f32[256]{0:T(256)} %param.16) | copy-start | bytes 3076
  6.6 217.6 %copy-start.4 = (s32[256,128]{1,0:T(8,128)S(1)}, s32[256,128]{1,0:T(8,128)}, u32[]{:S(2)}) copy-start(s32[256,128]{1,0:T(8,128)} %param.15) | copy-start | bytes 393220
  6.6 98.2 %reduce-scatter.3.cloned.1.call-start = ((), (), s32[]{:S(2)}) async-start(), calls=%async_computation.2 | async-start | bytes 1392640 | tf_op jit(solution)/shard_map/reduce_scatter | solution.py:62
  24.0 142.5 %reduce-scatter.5.cloned.1.call-start = ((), (), s32[]{:S(2)}) async-start(), calls=%async_computation.3 | async-start | bytes 589824 | tf_op jit(solution)/shard_map/reduce_scatter | solution.py:117
  133.6 148.9 %all-gather.3.cloned.1.call-start = ((), (), s32[]{:S(2)}) async-start(), calls=%async_computation.4 | async-start | bytes 4456448 | tf_op jit(solution)/shard_map/all_gather | solution.py:125
  289.5 16.3 %collective-permute-start = (f32[128,512]{1,0:T(8,128)S(1)}, f32[128,512]{1,0:T(8,128)S(1)}, u32[]{:S(2)}, u32[]{:S(2)}) collective-permute-start(f32[128,512]{1,0:T(8,128)S(1)} %constant_dynamic-slice_fusion.1), channel_id=1, source_target_pairs={{0,128},{128,0},{1,129},{129,1},{2,130},{130,2},{3,131},{131,3},{4... | collective-permute-start | bytes 786440 | tf_op jit(solution)/shard_map/ppermute | solution.py:16
Sparse Core Ops, SparseCore 0:
  24.1 80.6 reduce-scatter.2
  133.7 32.7 reduce-scatter.4
  224.2 58.2 all-gather.2
